TPU v7x, 32 devices: a whole 2x2x4 slice. The times are simulated.
32 devices in a mesh: rows: 2 (over x), cent: 16 (over z, y, core).
Axes of the slice: x: 2, y: 2, z: 4, core: 2. Of those that a mesh axis runs over, the one named last changes fastest.
Arguments:
- embeddings: bfloat16 [2048, 768], P(('rows', 'cent')), may hold values from -33 to 33
- centroids: bfloat16 [2048, 768], P('cent'), may hold values from -4 to 4
- group_length: int32 [2], P('rows'), may hold values from 256 to 1024, as said below
Outputs:
- new_centroids: bfloat16 [2048, 768], P('cent')
- new_moments: bfloat16 [2048, 768], P('cent')
- loglik: float32 [2048], P(('rows', 'cent'))
Inputs may be any that keep to these rules, and one draw needn't show every extreme that they name: Row group g uses its first group_length[g] of its 1024 row slots; at least one group uses all of them.
All inputs are finite; a program needn't handle non-finite values.
Results may differ from a plain program's by a relative error of at most 0.0047.
Values may be sent and summed in bfloat16 or wider, within the bound.
A program may use at most 64 MiB of HBM per device.

v0:
```python
import math

import jax
import jax.numpy as jnp
from jax import lax
from jax.sharding import PartitionSpec as P

score_factor = 3.0
prior_weight = 1.0
contract_rows = (((0,), (0,)), ((), ()))
contract_width = (((1,), (1,)), ((), ()))


def combined_all(part, axis, combine):
    gathered = jax.tree.map(lambda a: lax.all_gather(a, axis), part)

    def take(source):
        return jax.tree.map(lambda a: lax.dynamic_index_in_dim(a, source, 0, False), gathered)

    return lax.fori_loop(
        1, lax.axis_size(axis), lambda source, state: combine(state, take(source)), take(0)
    )


def scores(row_block, centroid_rows, squared_norm, factor):
    inner = lax.dot_general(
        row_block, centroid_rows, contract_width, preferred_element_type=jnp.float32
    )
    return factor * (inner - 0.5 * squared_norm[None, :])


def finish_totals(peaks, exp_sums):

    def combine(left_part, right_part):
        highest = jnp.maximum(left_part[0], right_part[0])
        joined = left_part[1] * jnp.exp(left_part[0] - highest) + right_part[1] * jnp.exp(
            right_part[0] - highest
        )
        return (highest, joined)

    peak_all, total_all = combined_all((peaks, exp_sums), "cent", combine)
    return peak_all + jnp.log(total_all)


def add_stats(row_piece, logits, piece_lse, valid_rows):
    responsibility = jnp.where(
        valid_rows[:, None], jnp.exp(logits - piece_lse[:, None]), 0.0
    ).astype(jnp.bfloat16)
    rows_wide = row_piece.astype(jnp.float32)
    squares = (rows_wide * rows_wide).astype(jnp.bfloat16)
    weighted = lax.dot_general(
        responsibility, row_piece, contract_rows, preferred_element_type=jnp.float32
    )
    moments = lax.dot_general(
        responsibility, squares, contract_rows, preferred_element_type=jnp.float32
    )
    weight_mass = jnp.sum(responsibility.astype(jnp.float32), axis=0)
    return (weighted, moments, weight_mass)


def shards(embeddings, centroids, group_length):
    row_count = embeddings.shape[0]
    width = embeddings.shape[1]
    factor = score_factor / math.sqrt(width)
    cent_wide = centroids.astype(jnp.float32)
    squared_norm = jnp.sum(cent_wide * cent_wide, axis=1)
    used_rows = group_length[0]
    offset = lax.axis_index("cent") * row_count
    own_positions = offset + jnp.arange(row_count, dtype=jnp.int32)
    own_valid = own_positions < used_rows
    logits = scores(
        lax.all_gather(embeddings, "cent", axis=0, tiled=True), centroids, squared_norm, factor
    )
    piece_peak = jnp.max(logits, axis=1)
    piece_total = jnp.sum(jnp.exp(logits - piece_peak[:, None]), axis=1)
    peaks = piece_peak
    exp_sums = piece_total
    peaks, exp_sums = (peaks, exp_sums)
    group_lse = finish_totals(peaks, exp_sums)
    row_piece = lax.all_gather(embeddings, "cent", axis=0, tiled=True)
    piece_count = row_piece.shape[0]
    logits = scores(row_piece, centroids, squared_norm, factor)
    positions = jnp.arange(piece_count, dtype=jnp.int32)
    weighted, moments, weight_mass = add_stats(row_piece, logits, group_lse, positions < used_rows)
    own_lse = lax.dynamic_slice_in_dim(group_lse, offset, row_count, 0)
    weighted, moments, weight_mass = lax.psum((weighted, moments, weight_mass), "rows")
    denominator = weight_mass[:, None] + prior_weight
    new_centroids = ((weighted + prior_weight * cent_wide) / denominator).astype(jnp.bfloat16)
    new_moments = ((moments + prior_weight) / denominator).astype(jnp.bfloat16)
    loglik = jnp.where(own_valid, own_lse, jnp.zeros_like(own_lse))
    return (new_centroids, new_moments, loglik)


def solution(mesh):
    return jax.shard_map(
        shards,
        mesh=mesh,
        in_specs=(P(("rows", "cent"), None), P("cent", None), P("rows")),
        out_specs=(P("cent", None), P("cent", None), P(("rows", "cent"))),
        check_vma=False,
    )
```

profile of v0, /device:TPU:0, one launch (start us, length us, event | category | flops | bytes accessed | tf_op | source)
XLA Modules:
  0.0 137.1 jit_solution(16626521679384497014)
XLA Ops:
  7.2 0.0 all-gather.4.cloned.1.call-start
  7.2 0.7 all-gather.4.cloned.1.call-update
  7.9 0.0 all-reduce.3.cloned.1.call-start
  8.6 1.0 fusion.2
  9.7 43.0 %all-gather.4.cloned.1.call-done = bf16[1024,768]{1,0:T(8,128)(2,1)} async-done(((bf16[64,768]{1,0:T(8,128)(2,1)}), bf16[1024,768]{1,0:T(8,128)(2,1)}) %all-gather.4.cloned.1.call-update) | async-done | bytes 1572880 | tf_op jit(solution)/shard_map/all_gather | solution.py:80
  52.6 2.1 %fusion.5 = (f32[1024]{0:T(1024)S(1)}, f32[1024,128]{0,1:T(8,128)S(1)}) fusion(f32[128]{0:T(128)S(1)} %broadcast_multiply_fusion, bf16[1024,768]{1,0:T(8,128)(2,1)} %all-gather.4.cloned.1.call-done, bf16[128,768]{1,0:T(8,128)(2,1)} %param.6), kind=kOutput, calls=%fused_computation.21 | convolution fusion | flops 201718784 | bytes 2298368 | tf_op jit(solution)/shard_map/dot_general | solution.py:26
  54.7 0.0 copy-start
  54.7 19.4 %all-gather = f32[16384]{0:T(1024)S(1)} all-gather(f32[1024]{0:T(1024)S(1)} %get-tuple-element.158), channel_id=2, replica_groups=mesh['rows'=2,'cent'=16] {'cent'}, dimensions={0}, use_global_device_ids=true | all-gather | bytes 69632 | tf_op jit(solution)/shard_map/all_gather | solution.py:15
  74.1 0.1 exponential_reduce_fusion
  74.2 17.6 %all-gather.1 = f32[16384]{0:T(1024)S(1)} all-gather(f32[1024]{0:T(1024)S(1)} %exponential_reduce_fusion), channel_id=3, replica_groups=mesh['rows'=2,'cent'=16] {'cent'}, dimensions={0}, use_global_device_ids=true | all-gather | bytes 69632 | tf_op jit(solution)/shard_map/all_gather | solution.py:15
  91.9 0.9 while.17
  92.8 0.2 convert_reduce_fusion
  93.0 0.0 copy-done
  93.0 1.2 fusion
  94.2 0.0 copy-start.1
  94.2 1.1 fusion.6
  95.3 0.0 all-reduce.3.cloned.1.call-update
  95.4 4.9 %psum.22 = f32[128]{0:T(128)S(1)} all-reduce(f32[128]{0:T(128)S(1)} %get-tuple-element.152), channel_id=1, replica_groups=mesh['rows'=2,'cent'=16] {'rows'}, use_global_device_ids=true, to_apply=%region_7.8 | all-reduce | flops 128 | bytes 1024 | tf_op jit(solution)/shard_map/psum | solution.py:86
  100.3 0.6 compare_select_fusion
  100.9 27.3 %all-reduce.3.cloned.1.call-done = (f32[128,768]{1,0:T(8,128)}, f32[128,768]{1,0:T(8,128)}) async-done(((f32[128,768]{1,0:T(8,128)}, f32[128,768]{1,0:T(8,128)}), (f32[128,768]{1,0:T(8,128)}, f32[128,768]{1,0:T(8,128)})) %all-reduce.3.cloned.1.call-update) | async-done | bytes 786448 | tf_op jit(solution)/shard_map/psum | solution.py:86
  128.2 0.0 copy-done.1
  128.2 2.0 %divide_convert_fusion = (bf16[128,768]{1,0:T(8,128)(2,1)}, bf16[128,768]{1,0:T(8,128)(2,1)}) fusion(f32[128,768]{1,0:T(8,128)} %get-tuple-element.149, f32[128]{0:T(128)S(1)} %broadcast_add_fusion, f32[128,768]{1,0:T(8,128)} %get-tuple-element.148, bf16[128,768]{1,0:T(8,128)(2,1)S(1)} %copy-done.1), kind=kLoop, calls=%fused_computation.15 | loop fusion | flops 688128 | bytes 1376768 | tf_op jit(solution)/shard_map/convert_element_type | solution.py:89
  (38 shorter events, 0.5 us)
Async XLA Ops:
  7.2 45.4 %all-gather.4.cloned.1.call-start = ((), (), s32[]{:S(2)}) async-start(), calls=%async_computation | async-start | bytes 1671168 | tf_op jit(solution)/shard_map/all_gather | solution.py:80
  7.9 120.3 %all-reduce.3.cloned.1.call-start = ((), (), s32[]{:S(2)}) async-start(), calls=%async_computation.1 | async-start | bytes 1572864 | tf_op jit(solution)/shard_map/psum | solution.py:86
  54.7 38.3 %copy-start = (bf16[1024,768]{1,0:T(8,128)(2,1)S(1)}, bf16[1024,768]{1,0:T(8,128)(2,1)}, u32[]{:S(2)}) copy-start(bf16[1024,768]{1,0:T(8,128)(2,1)} %all-gather.4.cloned.1.call-done) | copy-start | bytes 4718596
  94.2 34.0 %copy-start.1 = (bf16[128,768]{1,0:T(8,128)(2,1)S(1)}, bf16[128,768]{1,0:T(8,128)(2,1)}, u32[]{:S(2)}) copy-start(bf16[128,768]{1,0:T(8,128)(2,1)} %param.6) | copy-start | bytes 589828
Sparse Core Ops, SparseCore 0:
  10.3 42.3 all-gather.3
  95.5 32.7 all-reduce.2
where the time goes:
time: 137 us
  waiting for transfers between devices  71 us (52%)
  blocking collectives  42 us (31%)
  between operations  14.7 us (11%)
  matrix products  4.43 us (3%)
  other arithmetic  4.09 us (3%)
    all_gather x1, waiting for transfers between devices, shards(): row_piece = lax.all_gather(embeddings, 'cent', axis=0, tiled=True)  43 us
    all_gather x2, blocking collectives, combined_all(): gathered = jax.tree.map(lambda a: lax.all_gather(a, axis), part)  37 us
    psum x1, waiting for transfers between devices, shards(): lax.psum((weighted, moments, weight_mass), 'rows')  27.3 us
    psum x1, blocking collectives, shards(): lax.psum((weighted, moments, weight_mass), 'rows')  4.93 us
  transfers between devices with their start and end apart: 2, of which 2 were waited for; matrix products, arithmetic and copies ran while one was open for 1% of the time, Pallas kernels for 0%

commit v1 on v0

v1 whole, which is shorter than its diff:
```python
import functools
import math

import jax
import jax.numpy as jnp
from jax import lax
from jax.experimental import pallas as pl
from jax.experimental.pallas import tpu as pltpu
from jax.sharding import PartitionSpec as P

score_factor = 3.0
prior_weight = 1.0
MESH = pl.DeviceIdType.MESH
contract_width = (((1,), (1,)), ((), ()))
contract_rows = (((1,), (0,)), ((), ()))


def kernel(
    groups, shards, column_step,
    length_ref, emb_ref, cent_ref,
    cent_out, mom_out, lik_out,
    rows_all, squares, weights, parts, stats, masses,
    own_sem, z_send, z_recv, y_send, y_recv, c_send, c_recv,
    p_send, p_recv, s_send, s_recv, m_send, m_recv,
):
    g = lax.axis_index("rows")
    i = lax.axis_index("cent")
    row_count, width = emb_ref.shape
    cents = cent_ref.shape[0]
    total = shards * row_count
    line = shards // 4
    spot = lax.rem(i, 4)
    place = i // 4
    core = lax.rem(i, 2)
    core_peer = i + 1 - 2 * core
    y_peer = place * 4 + lax.rem(spot + 2, 4)
    factor = score_factor / math.sqrt(width)

    def along(step):
        return lax.rem(place + step, line) * 4 + spot

    def behind(step, where):
        return lax.rem(place + line - step, line) * 4 + where

    def across(step):
        return lax.rem(g + step, groups)

    barrier = pltpu.get_barrier_semaphore()
    peers = [(g, along(s)) for s in range(1, line)]
    peers += [(g, y_peer), (g, core_peer)]
    peers += [(across(s), i) for s in range(1, groups)]
    for peer in peers:
        pl.semaphore_signal(barrier, inc=1, device_id=peer, device_id_type=MESH)
    own = pltpu.make_async_copy(emb_ref, rows_all.at[i], own_sem)
    own.start()
    cent_wide = cent_ref[...].astype(jnp.float32)
    half_norm = 0.5 * jnp.sum(cent_wide * cent_wide, axis=1, keepdims=True)
    pl.semaphore_wait(barrier, len(peers))

    def send(src, dst, send_sem, recv_sem, peer):
        copy = pltpu.make_async_remote_copy(
            src_ref=src, dst_ref=dst, send_sem=send_sem, recv_sem=recv_sem,
            device_id=peer, device_id_type=MESH,
        )
        copy.start()
        return copy

    sent = []
    z_copies = {}
    y_copies = {}
    c_copies = {}
    mine = rows_all.at[i]
    y_copies[0] = send(emb_ref, mine, y_send.at[0], y_recv.at[0], (g, y_peer))
    for s in range(1, line):
        z_copies[s] = send(emb_ref, mine, z_send.at[s], z_recv.at[s], (g, along(s)))
    c_copies[0] = send(emb_ref, mine, c_send.at[0], c_recv.at[0], (g, core_peer))
    for s in range(1, line):
        z_copies[s].wait_recv()
        slot = rows_all.at[behind(s, spot)]
        y_copies[s] = send(slot, slot, y_send.at[s], y_recv.at[s], (g, y_peer))
        c_copies[s] = send(slot, slot, c_send.at[s], c_recv.at[s], (g, core_peer))
    for s in range(line):
        y_copies[s].wait_recv()
        slot = rows_all.at[behind(s, lax.rem(spot + 2, 4))]
        k = line + s
        c_copies[k] = send(slot, slot, c_send.at[k], c_recv.at[k], (g, core_peer))
    for k in range(2 * line):
        c_copies[k].wait_recv()
    own.wait()
    for copies in (z_copies, y_copies, c_copies):
        sent += list(copies.values())

    slots = max(1, min(shards, 512 // row_count))
    chunk = slots * row_count

    def score(k, carry):
        first = k * slots
        columns = k * chunk
        if not isinstance(k, int):
            columns = pl.multiple_of(columns, chunk)
        block = rows_all[pl.ds(first, slots)].reshape(chunk, width)
        inner = lax.dot_general(
            cent_ref[...], block, contract_width, preferred_element_type=jnp.float32
        )
        logits = factor * (inner - half_norm)
        peak = jnp.max(logits, axis=0, keepdims=True)
        weight = jnp.exp(logits - peak)
        weights[:, pl.ds(columns, chunk)] = weight
        parts[0, 0:1, pl.ds(columns, chunk)] = peak
        parts[0, 1:2, pl.ds(columns, chunk)] = jnp.sum(weight, axis=0, keepdims=True)
        return carry

    for k in range(shards // slots) if shards // slots <= 4 else ():
        score(k, 0)
    if shards // slots > 4:
        lax.fori_loop(0, shards // slots, score, 0)

    own_peak = parts[0, 0:1, :]

    def joined(part_list):
        highest = part_list[0][0]
        for peak, _ in part_list[1:]:
            highest = jnp.maximum(highest, peak)
        amount = None
        for peak, exp_sum in part_list:
            term = exp_sum * jnp.exp(peak - highest)
            amount = term if amount is None else amount + term
        return highest, amount

    def part(k):
        return parts[k, 0:1, :], parts[k, 1:2, :]

    hop = send(parts.at[0], parts.at[1], p_send.at[0], p_recv.at[0], (g, core_peer))

    def square(k, carry):
        wide = rows_all[k].astype(jnp.float32)
        squares[k] = (wide * wide).astype(jnp.bfloat16)
        return carry

    lax.fori_loop(0, shards, square, 0)
    hop.wait()
    peak, amount = joined([part(0), part(1)])
    parts[2, 0:1, :] = peak
    parts[2, 1:2, :] = amount
    hop = send(parts.at[2], parts.at[3], p_send.at[1], p_recv.at[1], (g, y_peer))
    hop.wait()
    peak, amount = joined([part(2), part(3)])
    parts[4, 0:1, :] = peak
    parts[4, 1:2, :] = amount
    hops = [
        send(parts.at[4], parts.at[4 + s], p_send.at[1 + s], p_recv.at[1 + s], (g, along(s)))
        for s in range(1, line)
    ]
    for hop in hops:
        hop.wait()
    peak, amount = joined([part(4 + s) for s in range(line)])
    lse = peak + jnp.log(amount)
    valid = lax.broadcasted_iota(jnp.int32, (1, total), 1) < length_ref[0]
    scale = jnp.where(valid, jnp.exp(own_peak - lse), 0.0)
    resp = (weights[...] * scale).astype(jnp.bfloat16)

    ones = jnp.ones((8, total), jnp.bfloat16)
    masses[g] = lax.dot_general(ones, resp, contract_width, preferred_element_type=jnp.float32)
    s_copies = {}
    for s in range(1, groups):
        sent.append(
            send(masses.at[g], masses.at[g], m_send.at[s], m_recv.at[s], (across(s), i))
        )
    m_copies = sent[len(sent) - (groups - 1):]
    pieces = 2 * (width // column_step)
    for k in range(pieces):
        left = (k // 2) * column_step
        source = rows_all if k % 2 == 0 else squares
        block = source[:, :, left:left + column_step].reshape(total, column_step)
        sums = lax.dot_general(resp, block, contract_rows, preferred_element_type=jnp.float32)
        stats[g, k] = sums.astype(jnp.bfloat16)
        for s in range(1, groups):
            s_copies[k, s] = send(
                stats.at[g, k], stats.at[g, k], s_send.at[k, s], s_recv.at[k, s], (across(s), i)
            )

    own_lik = jnp.where(valid, lse, 0.0)
    pick = own_lik[:, 0:row_count]
    for j in range(1, shards):
        pick = jnp.where(i == j, own_lik[:, j * row_count:(j + 1) * row_count], pick)
    lik_out[...] = pick

    for copy in m_copies:
        copy.wait_recv()
    mass = masses[0, 0:1, :]
    for r in range(1, groups):
        mass = mass + masses[r, 0:1, :]
    inverse = 1.0 / (mass + prior_weight)
    inverse = jnp.transpose(jnp.broadcast_to(inverse, (cents, cents)))[:, 0:1]
    for k in range(pieces):
        for s in range(1, groups):
            s_copies[k, s].wait_recv()
        left = (k // 2) * column_step
        sums = stats[0, k].astype(jnp.float32)
        for r in range(1, groups):
            sums = sums + stats[r, k].astype(jnp.float32)
        if k % 2 == 0:
            sums = sums + prior_weight * cent_ref[:, left:left + column_step].astype(jnp.float32)
            cent_out[:, left:left + column_step] = (sums * inverse).astype(jnp.bfloat16)
        else:
            mom_out[:, left:left + column_step] = ((sums + prior_weight) * inverse).astype(
                jnp.bfloat16
            )
    for copy in sent + list(s_copies.values()):
        copy.wait_send()


def solution(mesh):
    groups = mesh.shape["rows"]
    shards = mesh.shape["cent"]
    line = shards // 4

    def step(embeddings, centroids, group_length):
        row_count, width = embeddings.shape
        cents = centroids.shape[0]
        total = row_count * shards
        column_step = 256 if width % 256 == 0 else width
        pieces = 2 * (width // column_step)
        vmem = pl.BlockSpec(memory_space=pltpu.VMEM)
        dma = pltpu.SemaphoreType.DMA
        new_centroids, new_moments, loglik = pl.pallas_call(
            functools.partial(kernel, groups, shards, column_step),
            out_shape=(
                jax.ShapeDtypeStruct((cents, width), jnp.bfloat16),
                jax.ShapeDtypeStruct((cents, width), jnp.bfloat16),
                jax.ShapeDtypeStruct((1, row_count), jnp.float32),
            ),
            in_specs=[pl.BlockSpec(memory_space=pltpu.SMEM), vmem, vmem],
            out_specs=(vmem, vmem, vmem),
            scratch_shapes=[
                pltpu.VMEM((shards, row_count, width), jnp.bfloat16),
                pltpu.VMEM((shards, row_count, width), jnp.bfloat16),
                pltpu.VMEM((cents, total), jnp.float32),
                pltpu.VMEM((4 + line, 2, total), jnp.float32),
                pltpu.VMEM((groups, pieces, cents, column_step), jnp.bfloat16),
                pltpu.VMEM((groups, 8, cents), jnp.float32),
                dma, dma((line,)), dma((line,)), dma((line,)), dma((line,)),
                dma((2 * line,)), dma((2 * line,)),
                dma((1 + line,)), dma((1 + line,)),
                dma((pieces, groups)), dma((pieces, groups)),
                dma((groups,)), dma((groups,)),
            ],
            compiler_params=pltpu.CompilerParams(
                collective_id=0, has_side_effects=True, vmem_limit_bytes=56 * 1024 * 1024
            ),
            name="soft_em",
        )(group_length, embeddings, centroids)
        return new_centroids, new_moments, loglik.reshape(row_count)

    return jax.shard_map(
        step,
        mesh=mesh,
        in_specs=(P(("rows", "cent"), None), P("cent", None), P("rows")),
        out_specs=(P("cent", None), P("cent", None), P(("rows", "cent"))),
        check_vma=False,
    )
```

time: 137 us -> 45.4 us (0.33)
  waiting for transfers between devices: 71 us -> 0 us
  blocking collectives: 42 us -> 0 us
  Pallas kernels: 0 us -> 41.1 us
  between operations: 14.7 us -> 1.3 us
  matrix products: 4.43 us -> 0 us
  other arithmetic: 4.09 us -> 0 us
  local copies, waits for them, and re-layouts: 0.27 us -> 2.85 us
    all_gather x1 -> x0, waiting for transfers between devices: 43 us -> none  [shards(): row_piece = lax.all_gather(embeddings, 'cent', axis=0, tiled=True)]
    pallas_call x0 -> x1, Pallas kernels: none -> 41.1 us  [step(): pl.pallas_call(functools.partial(kernel, groups, shards, column_step), ou...]
    all_gather x2 -> x0, blocking collectives: 37 us -> none  [combined_all(): gathered = jax.tree.map(lambda a: lax.all_gather(a, axis), part)]
    psum x1 -> x0, waiting for transfers between devices: 27.3 us -> none  [shards(): lax.psum((weighted, moments, weight_mass), 'rows')]
    psum x1 -> x0, blocking collectives: 4.93 us -> none  [shards(): lax.psum((weighted, moments, weight_mass), 'rows')]
    dot_general x3 -> x0, matrix products: 4.43 us -> none  [the longest x1 2.06 us: scores(): lax.dot_general(row_block, centroid_rows, contract_width, preferred_eleme...]
    unnamed x4 -> x7, local copies, waits for them, and re-layouts: 0.01 us -> 2.85 us
    convert_element_type x1 -> x0, other arithmetic: 1.99 us -> none  [shards(): new_moments = ((moments + prior_weight) / denominator).astype(jnp.bfloat16)]
  transfers between devices with their start and end apart: 2 -> 0, of which waited for: 2 -> 0; matrix products, arithmetic and copies ran while one was open for 1% -> 0% of each run, Pallas kernels for 0% -> 0%
where the time goes in v1:
time: 45.4 us; the launch traced here: 45.2 us
  Pallas kernels  41.1 us (91%)
  local copies, waits for them, and re-layouts  2.85 us (6%)
  between operations  1.3 us (3%)
    pallas_call x1, Pallas kernels, step(): pl.pallas_call(functools.partial(kernel, groups, shards, column_step), ou...  41.1 us
    unnamed x7, local copies, waits for them, and re-layouts  2.85 us

profile of v1, /device:TPU:0, one launch (start us, length us, event | category | flops | bytes accessed | tf_op | source)
XLA Modules:
  0.0 45.2 jit_solution(6742359067669081429)
XLA Ops:
  1.3 41.1 %soft_em.1 = (bf16[128,768]{1,0:T(8,128)(2,1)}, bf16[128,768]{1,0:T(8,128)(2,1)}, f32[1,64]{1,0:T(1,128)}) custom-call(s32[1]{0:T(128)S(6)} %copy.9.length_ref, bf16[64,768]{1,0:T(8,128)(2,1)} %emb_ref.1, bf16[128,768]{1,0:T(8,128)(2,1)} %cent_ref.1), custom_call_target="tpu_custom_call" | custom-call | tf_op jit(solution)/shard_map/soft_em/pallas_call | solution.py:226
  42.4 0.0 copy-start
  42.4 1.7 %copy.10 = bf16[128,768]{1,0:T(8,128)(2,1)} copy(bf16[128,768]{1,0:T(8,128)(2,1)} %get-tuple-element.12) | data formatting | bytes 393216
  44.0 0.0 copy-done
  44.0 0.0 copy-start.1
  44.0 0.7 %copy.11 = bf16[128,768]{1,0:T(8,128)(2,1)} copy(bf16[128,768]{1,0:T(8,128)(2,1)S(1)} %copy-done) | data formatting | bytes 393216
  44.7 0.0 copy-done.1
  44.7 0.5 %copy.12 = f32[64]{0:T(128)} copy(f32[64]{0:T(128)S(1)} %bitcast.1) | data formatting | bytes 512
Async XLA Ops:
  42.4 1.7 %copy-start = (bf16[128,768]{1,0:T(8,128)(2,1)S(1)}, bf16[128,768]{1,0:T(8,128)(2,1)}, u32[]{:S(2)}) copy-start(bf16[128,768]{1,0:T(8,128)(2,1)} %get-tuple-element.13) | copy-start | bytes 589828
  44.0 0.7 %copy-start.1 = (f32[1,64]{1,0:T(1,128)S(1)}, f32[1,64]{1,0:T(1,128)}, u32[]{:S(2)}) copy-start(f32[1,64]{1,0:T(1,128)} %get-tuple-element.8) | copy-start | bytes 772

commit v2 on v1

v2 whole, which is shorter than its diff:
```python
import functools
import math

import jax
import jax.numpy as jnp
from jax import lax
from jax.experimental import pallas as pl
from jax.experimental.pallas import tpu as pltpu
from jax.sharding import PartitionSpec as P

score_factor = 3.0
prior_weight = 1.0
MESH = pl.DeviceIdType.MESH
contract_width = (((1,), (1,)), ((), ()))
contract_rows = (((1,), (0,)), ((), ()))


def kernel(
    groups, shards, column_step, split,
    length_ref, emb_hbm, cent_hbm,
    cent_out, mom_out, lik_out,
    cent_ref, rows_all, squares, weights, parts, stats, masses,
    own_sem, cent_sem, z_send, z_recv, y_send, y_recv, c_send, c_recv,
    p_send, p_recv, s_send, s_recv, m_send, m_recv,
):
    g = lax.axis_index("rows")
    i = lax.axis_index("cent")
    row_count, width = emb_hbm.shape
    cents = cent_ref.shape[0]
    total = shards * row_count
    piece_rows = row_count // split
    line = shards // 4
    spot = lax.rem(i, 4)
    place = i // 4
    core = lax.rem(i, 2)
    core_peer = i + 1 - 2 * core
    y_spot = lax.rem(spot + 2, 4)
    y_peer = place * 4 + y_spot
    factor = score_factor / math.sqrt(width)

    def across(step):
        return lax.rem(g + step, groups)

    def signal(peer):
        pl.semaphore_signal(barrier, inc=1, device_id=peer, device_id_type=MESH)

    barrier = pltpu.get_barrier_semaphore()
    for peer in [(g, y_peer), (g, core_peer)] + [(across(s), i) for s in range(1, groups)]:
        signal(peer)
    has_right = place < line - 1
    has_left = place > 0
    pl.when(has_right)(lambda: signal((g, i + 4)))
    pl.when(has_left)(lambda: signal((g, i - 4)))
    own = [
        pltpu.make_async_copy(
            emb_hbm.at[pl.ds(h * piece_rows, piece_rows)], rows_all.at[i * split + h], own_sem.at[h]
        )
        for h in range(split)
    ]
    for copy in own:
        copy.start()
    cent_copy = pltpu.make_async_copy(cent_hbm, cent_ref, cent_sem)
    cent_copy.start()
    for copy in own:
        copy.wait()
    sides = has_right.astype(jnp.int32) + has_left.astype(jnp.int32)
    pl.semaphore_wait(barrier, 1 + groups + sides)

    def describe(src, dst, send_sem, recv_sem, peer):
        return pltpu.make_async_remote_copy(
            src_ref=src, dst_ref=dst, send_sem=send_sem, recv_sem=recv_sem,
            device_id=peer, device_id_type=MESH,
        )

    def send(*spec):
        copy = describe(*spec)
        copy.start()
        return copy

    def z_copy(unit, way, s, h):
        slot = rows_all.at[unit]
        peer = (g, i + 4 if way == 0 else i - 4)
        return describe(slot, slot, z_send.at[way, s, h], z_recv.at[way, s, h], peer)

    def y_copy(unit, k, h):
        slot = rows_all.at[unit]
        return describe(slot, slot, y_send.at[k, h], y_recv.at[k, h], (g, y_peer))

    def c_copy(unit, k, h):
        slot = rows_all.at[unit]
        return describe(slot, slot, c_send.at[k, h], c_recv.at[k, h], (g, core_peer))

    def square(unit):
        wide = rows_all[unit].astype(jnp.float32)
        squares[unit] = (wide * wide).astype(jnp.bfloat16)

    steps = 2 * line - 1
    order = [(way, s) for s in range(1, line) for way in range(2)]

    def present(way, s):
        return place >= s if way == 0 else place + s < line

    def unit_of(way, s, where, h):
        source = place - s if way == 0 else place + s
        return (source * 4 + where) * split + h

    for h in range(split):
        unit = i * split + h
        pl.when(has_right)(lambda: z_copy(unit, 0, 1, h).start())
        pl.when(has_left)(lambda: z_copy(unit, 1, 1, h).start())
        y_copy(unit, 0, h).start()
        c_copy(unit, 0, h).start()
    for h in range(split):
        square(i * split + h)
    for k, (way, s) in enumerate(order, 1):
        for h in range(split):
            def relay():
                unit = unit_of(way, s, spot, h)
                z_copy(unit, way, s, h).wait_recv()
                onward = has_right if way == 0 else has_left
                if s + 1 < line:
                    pl.when(onward)(lambda: z_copy(unit, way, s + 1, h).start())
                y_copy(unit, k, h).start()
                c_copy(unit, k, h).start()
                square(unit)

            pl.when(present(way, s))(relay)
    for h in range(split):
        unit = unit_of(0, 0, y_spot, h)
        y_copy(unit, 0, h).wait_recv()
        c_copy(unit, steps, h).start()
        square(unit)
    for k, (way, s) in enumerate(order, 1):
        for h in range(split):
            def pass_on():
                unit = unit_of(way, s, y_spot, h)
                y_copy(unit, k, h).wait_recv()
                c_copy(unit, steps + k, h).start()
                square(unit)

            pl.when(present(way, s))(pass_on)
    other = spot + 1 - 2 * core
    for j, where in enumerate((other, lax.rem(other + 2, 4))):
        for h in range(split):
            unit = unit_of(0, 0, where, h)
            c_copy(unit, j * steps, h).wait_recv()
            square(unit)
        for k, (way, s) in enumerate(order, 1):
            for h in range(split):
                def take():
                    unit = unit_of(way, s, where, h)
                    c_copy(unit, j * steps + k, h).wait_recv()
                    square(unit)

                pl.when(present(way, s))(take)
    sent = []
    cent_copy.wait()
    cent_wide = cent_ref[...].astype(jnp.float32)
    half_norm = 0.5 * jnp.sum(cent_wide * cent_wide, axis=1, keepdims=True)

    slots = split * max(1, min(shards, 512 // row_count))
    chunk = slots * piece_rows
    chunks = shards * split // slots

    def score(k, carry):
        first = k * slots
        columns = k * chunk
        if not isinstance(k, int):
            columns = pl.multiple_of(columns, chunk)
        block = rows_all[pl.ds(first, slots)].reshape(chunk, width)
        inner = lax.dot_general(
            cent_ref[...], block, contract_width, preferred_element_type=jnp.float32
        )
        logits = factor * (inner - half_norm)
        peak = jnp.max(logits, axis=0, keepdims=True)
        weight = jnp.exp(logits - peak)
        weights[:, pl.ds(columns, chunk)] = weight
        parts[0, 0:1, pl.ds(columns, chunk)] = peak
        parts[0, 1:2, pl.ds(columns, chunk)] = jnp.sum(weight, axis=0, keepdims=True)
        return carry

    for k in range(chunks) if chunks <= 4 else ():
        score(k, 0)
    if chunks > 4:
        lax.fori_loop(0, chunks, score, 0)

    own_peak = parts[0, 0:1, :]

    def joined(part_list):
        highest = part_list[0][0]
        for peak, _ in part_list[1:]:
            highest = jnp.maximum(highest, peak)
        amount = None
        for peak, exp_sum in part_list:
            term = exp_sum * jnp.exp(peak - highest)
            amount = term if amount is None else amount + term
        return highest, amount

    def part(k):
        return parts[k, 0:1, :], parts[k, 1:2, :]

    hop = send(parts.at[0], parts.at[1], p_send.at[0], p_recv.at[0], (g, core_peer))

    hop.wait()
    peak, amount = joined([part(0), part(1)])
    parts[2, 0:1, :] = peak
    parts[2, 1:2, :] = amount
    hops = []
    for k in range(2 * line - 1, 0, -1):
        peer = lax.rem(place + k // 2, line) * 4 + lax.rem(spot + 2 * (k % 2), 4)
        hops.append(send(parts.at[2], parts.at[2 + k], p_send.at[k], p_recv.at[k], (g, peer)))
    for hop in hops:
        hop.wait_recv()
    sent += hops
    peak, amount = joined([part(2 + k) for k in range(2 * line)])
    lse = peak + jnp.log(amount)
    valid = lax.broadcasted_iota(jnp.int32, (1, total), 1) < length_ref[0]
    scale = jnp.where(valid, jnp.exp(own_peak - lse), 0.0)
    resp = (weights[...] * scale).astype(jnp.bfloat16)

    ones = jnp.ones((8, total), jnp.bfloat16)
    masses[g] = lax.dot_general(ones, resp, contract_width, preferred_element_type=jnp.float32)
    s_copies = {}
    for s in range(1, groups):
        sent.append(
            send(masses.at[g], masses.at[g], m_send.at[s], m_recv.at[s], (across(s), i))
        )
    m_copies = sent[len(sent) - (groups - 1):]
    pieces = 2 * (width // column_step)
    for k in range(pieces):
        left = (k // 2) * column_step
        source = rows_all if k % 2 == 0 else squares
        block = source[:, :, left:left + column_step].reshape(total, column_step)
        sums = lax.dot_general(resp, block, contract_rows, preferred_element_type=jnp.float32)
        stats[g, k] = sums.astype(jnp.bfloat16)
        for s in range(1, groups):
            s_copies[k, s] = send(
                stats.at[g, k], stats.at[g, k], s_send.at[k, s], s_recv.at[k, s], (across(s), i)
            )

    own_lik = jnp.where(valid, lse, 0.0)
    pick = own_lik[:, 0:row_count]
    for j in range(1, shards):
        pick = jnp.where(i == j, own_lik[:, j * row_count:(j + 1) * row_count], pick)
    lik_out[...] = pick

    for copy in m_copies:
        copy.wait_recv()
    mass = masses[0, 0:1, :]
    for r in range(1, groups):
        mass = mass + masses[r, 0:1, :]
    inverse = 1.0 / (mass + prior_weight)
    inverse = jnp.transpose(jnp.broadcast_to(inverse, (cents, cents)))[:, 0:1]
    for k in range(pieces):
        for s in range(1, groups):
            s_copies[k, s].wait_recv()
        left = (k // 2) * column_step
        sums = stats[0, k].astype(jnp.float32)
        for r in range(1, groups):
            sums = sums + stats[r, k].astype(jnp.float32)
        if k % 2 == 0:
            sums = sums + prior_weight * cent_ref[:, left:left + column_step].astype(jnp.float32)
            cent_out[:, left:left + column_step] = (sums * inverse).astype(jnp.bfloat16)
        else:
            mom_out[:, left:left + column_step] = ((sums + prior_weight) * inverse).astype(
                jnp.bfloat16
            )
    for h in range(split):
        unit = i * split + h
        pl.when(has_right)(lambda: z_copy(unit, 0, 1, h).wait_send())
        pl.when(has_left)(lambda: z_copy(unit, 1, 1, h).wait_send())
        y_copy(unit, 0, h).wait_send()
        c_copy(unit, 0, h).wait_send()
        c_copy(unit_of(0, 0, y_spot, h), steps, h).wait_send()
    for k, (way, s) in enumerate(order, 1):
        for h in range(split):
            def finish():
                unit = unit_of(way, s, spot, h)
                onward = has_right if way == 0 else has_left
                if s + 1 < line:
                    pl.when(onward)(lambda: z_copy(unit, way, s + 1, h).wait_send())
                y_copy(unit, k, h).wait_send()
                c_copy(unit, k, h).wait_send()
                c_copy(unit_of(way, s, y_spot, h), steps + k, h).wait_send()

            pl.when(present(way, s))(finish)
    for copy in sent + list(s_copies.values()):
        copy.wait_send()


def solution(mesh):
    groups = mesh.shape["rows"]
    shards = mesh.shape["cent"]
    line = shards // 4

    def step(embeddings, centroids, group_length):
        row_count, width = embeddings.shape
        cents = centroids.shape[0]
        total = row_count * shards
        column_step = 256 if width % 256 == 0 else width
        pieces = 2 * (width // column_step)
        split = 2 if row_count % 32 == 0 else 1
        vmem = pl.BlockSpec(memory_space=pltpu.VMEM)
        hbm = pl.BlockSpec(memory_space=pltpu.HBM)
        held = 4 * total * width + 4 * cents * total + 2 * (groups * 2 + 1) * cents * width
        steps = 2 * line - 1
        dma = pltpu.SemaphoreType.DMA
        new_centroids, new_moments, loglik = pl.pallas_call(
            functools.partial(kernel, groups, shards, column_step, split),
            out_shape=(
                jax.ShapeDtypeStruct((cents, width), jnp.bfloat16),
                jax.ShapeDtypeStruct((cents, width), jnp.bfloat16),
                jax.ShapeDtypeStruct((1, row_count), jnp.float32),
            ),
            in_specs=[pl.BlockSpec(memory_space=pltpu.SMEM), hbm, hbm],
            out_specs=(vmem, vmem, vmem),
            scratch_shapes=[
                pltpu.VMEM((cents, width), jnp.bfloat16),
                pltpu.VMEM((shards * split, row_count // split, width), jnp.bfloat16),
                pltpu.VMEM((shards * split, row_count // split, width), jnp.bfloat16),
                pltpu.VMEM((cents, total), jnp.float32),
                pltpu.VMEM((2 + 2 * line, 2, total), jnp.float32),
                pltpu.VMEM((groups, pieces, cents, column_step), jnp.bfloat16),
                pltpu.VMEM((groups, 8, cents), jnp.float32),
                dma((split,)), dma, dma((2, line, split)), dma((2, line, split)),
                dma((steps, split)), dma((steps, split)),
                dma((2 * steps, split)), dma((2 * steps, split)),
                dma((2 * line,)), dma((2 * line,)),
                dma((pieces, groups)), dma((pieces, groups)),
                dma((groups,)), dma((groups,)),
            ],
            compiler_params=pltpu.CompilerParams(
                collective_id=0, has_side_effects=True, vmem_limit_bytes=2 * held + 4 * 1024 * 1024
            ),
            name="soft_em",
        )(group_length, embeddings, centroids)
        return new_centroids, new_moments, loglik.reshape(row_count)

    return jax.shard_map(
        step,
        mesh=mesh,
        in_specs=(P(("rows", "cent"), None), P("cent", None), P("rows")),
        out_specs=(P("cent", None), P("cent", None), P(("rows", "cent"))),
        check_vma=False,
    )
```

time: 45.4 us -> 40.7 us (0.90)
  Pallas kernels: 41.1 us -> 35.6 us
  local copies, waits for them, and re-layouts: 2.85 us -> 3.68 us
    pallas_call x1, Pallas kernels: 41.1 us -> 35.6 us  [step(): pl.pallas_call(functools.partial(kernel, groups, shards, column_step, spl...]
    unnamed x7, local copies, waits for them, and re-layouts: 2.85 us -> 3.68 us
where the time goes in v2:
time: 40.7 us; the launch traced here: 40.6 us
  Pallas kernels  35.6 us (87%)
  local copies, waits for them, and re-layouts  3.68 us (9%)
  between operations  1.3 us (3%)
    pallas_call x1, Pallas kernels, step(): pl.pallas_call(functools.partial(kernel, groups, shards, column_step, spl...  35.6 us
    unnamed x7, local copies, waits for them, and re-layouts  3.68 us

profile of v2, /device:TPU:0, one launch (start us, length us, event | category | flops | bytes accessed | tf_op | source)
XLA Modules:
  0.0 40.6 jit_solution(2015535701581476352)
XLA Ops:
  1.3 0.0 copy-start
  1.3 0.9 %copy-done = bf16[128,768]{1,0:T(8,128)(2,1)S(1)} copy-done((bf16[128,768]{1,0:T(8,128)(2,1)S(1)}, bf16[128,768]{1,0:T(8,128)(2,1)}, u32[]{:S(2)}) %copy-start) | copy-done | bytes 196632
  2.2 0.0 copy-start.1
  2.2 0.9 %copy-done.1 = bf16[64,768]{1,0:T(8,128)(2,1)S(1)} copy-done((bf16[64,768]{1,0:T(8,128)(2,1)S(1)}, bf16[64,768]{1,0:T(8,128)(2,1)}, u32[]{:S(2)}) %copy-start.1) | copy-done | bytes 98328
  3.1 35.6 %soft_em.1 = (bf16[128,768]{1,0:T(8,128)(2,1)S(1)}, bf16[128,768]{1,0:T(8,128)(2,1)S(1)}, f32[1,64]{1,0:T(1,128)S(1)}) custom-call(s32[1]{0:T(128)S(6)} %copy.9.length_ref, bf16[64,768]{1,0:T(8,128)(2,1)S(1)} %copy-done.1, bf16[128,768]{1,0:T(8,128)(2,1)S(1)} %copy-done), custom_call_target="tpu_custom_call" | custom-call | tf_op jit(solution)/shard_map/soft_em/pallas_call | solution.py:308
  38.7 0.7 %copy.10 = bf16[128,768]{1,0:T(8,128)(2,1)} copy(bf16[128,768]{1,0:T(8,128)(2,1)S(1)} %get-tuple-element.12) | data formatting | bytes 393216
  39.4 0.7 %copy.11 = bf16[128,768]{1,0:T(8,128)(2,1)} copy(bf16[128,768]{1,0:T(8,128)(2,1)S(1)} %get-tuple-element.13) | data formatting | bytes 393216
  40.1 0.5 %copy.12 = f32[64]{0:T(128)} copy(f32[64]{0:T(128)S(1)} %bitcast.1) | data formatting | bytes 512
Async XLA Ops:
  1.3 0.9 %copy-start = (bf16[128,768]{1,0:T(8,128)(2,1)S(1)}, bf16[128,768]{1,0:T(8,128)(2,1)}, u32[]{:S(2)}) copy-start(bf16[128,768]{1,0:T(8,128)(2,1)} %cent_hbm.1) | copy-start | bytes 589828
  2.2 0.9 %copy-start.1 = (bf16[64,768]{1,0:T(8,128)(2,1)S(1)}, bf16[64,768]{1,0:T(8,128)(2,1)}, u32[]{:S(2)}) copy-start(bf16[64,768]{1,0:T(8,128)(2,1)} %emb_hbm.1) | copy-start | bytes 294916

commit v3 on v2

--- a/solution.py
+++ b/solution.py
@@ -333,7 +333,7 @@
                 collective_id=0, has_side_effects=True, vmem_limit_bytes=2 * held + 4 * 1024 * 1024
             ),
             name="soft_em",
-        )(group_length, embeddings, centroids)
+        )(group_length, pltpu.with_memory_space_constraint(embeddings, pltpu.HBM), pltpu.with_memory_space_constraint(centroids, pltpu.HBM))
         return new_centroids, new_moments, loglik.reshape(row_count)
 
     return jax.shard_map(

time: 40.7 us -> 39 us (0.958)
  local copies, waits for them, and re-layouts: 3.68 us -> 1.87 us
    unnamed x7 -> x3, local copies, waits for them, and re-layouts: 3.68 us -> 1.87 us
where the time goes in v3:
time: 39 us; the launch traced here: 38.8 us
  Pallas kernels  35.7 us (92%)
  local copies, waits for them, and re-layouts  1.87 us (5%)
  between operations  1.29 us (3%)
    pallas_call x1, Pallas kernels, step(): pl.pallas_call(functools.partial(kernel, groups, shards, column_step, spl...  35.7 us
    unnamed x3, local copies, waits for them, and re-layouts  1.87 us

profile of v3, /device:TPU:0, one launch (start us, length us, event | category | flops | bytes accessed | tf_op | source)
XLA Modules:
  0.0 38.8 jit_solution(809057877838770642)
XLA Ops:
  1.3 35.7 %soft_em.1 = (bf16[128,768]{1,0:T(8,128)(2,1)S(1)}, bf16[128,768]{1,0:T(8,128)(2,1)S(1)}, f32[1,64]{1,0:T(1,128)S(1)}) custom-call(s32[1]{0:T(128)S(6)} %copy.9.length_ref, bf16[64,768]{1,0:T(8,128)(2,1)} %emb_hbm.1, bf16[128,768]{1,0:T(8,128)(2,1)} %cent_hbm.1), custom_call_target="tpu_custom_call" | custom-call | tf_op jit(solution)/shard_map/soft_em/pallas_call | solution.py:308
  36.9 0.7 %copy.10 = bf16[128,768]{1,0:T(8,128)(2,1)} copy(bf16[128,768]{1,0:T(8,128)(2,1)S(1)} %get-tuple-element.12) | data formatting | bytes 393216
  37.6 0.7 %copy.11 = bf16[128,768]{1,0:T(8,128)(2,1)} copy(bf16[128,768]{1,0:T(8,128)(2,1)S(1)} %get-tuple-element.13) | data formatting | bytes 393216
  38.3 0.5 %copy.12 = f32[64]{0:T(128)} copy(f32[64]{0:T(128)S(1)} %bitcast.1) | data formatting | bytes 512

commit v4 on v3

--- a/solution.py
+++ b/solution.py
@@ -18,7 +18,7 @@
 def kernel(
     groups, shards, column_step, split,
     length_ref, emb_hbm, cent_hbm,
-    cent_out, mom_out, lik_out,
+    cent_out, mom_out, lik_out, inverse_out,
     cent_ref, rows_all, squares, weights, parts, stats, masses,
     own_sem, cent_sem, z_send, z_recv, y_send, y_recv, c_send, c_recv,
     p_send, p_recv, s_send, s_recv, m_send, m_recv,
@@ -250,7 +250,7 @@
     for r in range(1, groups):
         mass = mass + masses[r, 0:1, :]
     inverse = 1.0 / (mass + prior_weight)
-    inverse = jnp.transpose(jnp.broadcast_to(inverse, (cents, cents)))[:, 0:1]
+    inverse_out[...] = jnp.transpose(jnp.broadcast_to(inverse, (cents, cents)))
     for k in range(pieces):
         for s in range(1, groups):
             s_copies[k, s].wait_recv()
@@ -260,11 +260,9 @@
             sums = sums + stats[r, k].astype(jnp.float32)
         if k % 2 == 0:
             sums = sums + prior_weight * cent_ref[:, left:left + column_step].astype(jnp.float32)
-            cent_out[:, left:left + column_step] = (sums * inverse).astype(jnp.bfloat16)
+            cent_out[:, left:left + column_step] = sums
         else:
-            mom_out[:, left:left + column_step] = ((sums + prior_weight) * inverse).astype(
-                jnp.bfloat16
-            )
+            mom_out[:, left:left + column_step] = sums + prior_weight
     for h in range(split):
         unit = i * split + h
         pl.when(has_right)(lambda: z_copy(unit, 0, 1, h).wait_send())
@@ -305,15 +303,16 @@
         held = 4 * total * width + 4 * cents * total + 2 * (groups * 2 + 1) * cents * width
         steps = 2 * line - 1
         dma = pltpu.SemaphoreType.DMA
-        new_centroids, new_moments, loglik = pl.pallas_call(
+        cent_sums, moment_sums, loglik, inverse = pl.pallas_call(
             functools.partial(kernel, groups, shards, column_step, split),
             out_shape=(
-                jax.ShapeDtypeStruct((cents, width), jnp.bfloat16),
-                jax.ShapeDtypeStruct((cents, width), jnp.bfloat16),
+                jax.ShapeDtypeStruct((cents, width), jnp.float32),
+                jax.ShapeDtypeStruct((cents, width), jnp.float32),
                 jax.ShapeDtypeStruct((1, row_count), jnp.float32),
+                jax.ShapeDtypeStruct((cents, cents), jnp.float32),
             ),
             in_specs=[pl.BlockSpec(memory_space=pltpu.SMEM), hbm, hbm],
-            out_specs=(vmem, vmem, vmem),
+            out_specs=(vmem, vmem, vmem, vmem),
             scratch_shapes=[
                 pltpu.VMEM((cents, width), jnp.bfloat16),
                 pltpu.VMEM((shards * split, row_count // split, width), jnp.bfloat16),
@@ -334,6 +333,8 @@
             ),
             name="soft_em",
         )(group_length, pltpu.with_memory_space_constraint(embeddings, pltpu.HBM), pltpu.with_memory_space_constraint(centroids, pltpu.HBM))
+        new_centroids = (cent_sums * inverse[:, 0:1]).astype(jnp.bfloat16)
+        new_moments = (moment_sums * inverse[:, 0:1]).astype(jnp.bfloat16)
         return new_centroids, new_moments, loglik.reshape(row_count)
 
     return jax.shard_map(

time: 39 us -> 38.6 us (0.990)
  local copies, waits for them, and re-layouts: 1.87 us -> 0.61 us
  other arithmetic: 0 us -> 0.87 us
    unnamed x3 -> x1, local copies, waits for them, and re-layouts: 1.87 us -> 0.51 us
    convert_element_type x0 -> x1, other arithmetic: none -> 0.87 us  [step(): new_moments = (moment_sums * inverse[:, 0:1]).astype(jnp.bfloat16)]
where the time goes in v4:
time: 38.6 us; the launch traced here: 38.4 us
  Pallas kernels  35.7 us (92%)
  between operations  1.29 us (3%)
  other arithmetic  0.87 us (2%)
  local copies, waits for them, and re-layouts  0.61 us (2%)
    pallas_call x1, Pallas kernels, step(): pl.pallas_call(functools.partial(kernel, groups, shards, column_step, spl...  35.7 us
    convert_element_type x1, other arithmetic, step(): new_moments = (moment_sums * inverse[:, 0:1]).astype(jnp.bfloat16)  0.87 us

profile of v4, /device:TPU:0, one launch (start us, length us, event | category | flops | bytes accessed | tf_op | source)
XLA Modules:
  0.0 38.4 jit_solution(15215355789312995771)
XLA Ops:
  1.3 35.7 %soft_em.1 = (f32[128,768]{1,0:T(8,128)S(1)}, f32[128,768]{1,0:T(8,128)S(1)}, f32[1,64]{1,0:T(1,128)S(1)}, f32[128,128]{1,0:T(8,128)S(1)}) custom-call(s32[1]{0:T(128)S(6)} %copy.7.length_ref, bf16[64,768]{1,0:T(8,128)(2,1)} %emb_hbm.1, bf16[128,768]{1,0:T(8,128)(2,1)} %cent_hbm.1), custom_call_target="tpu_custom_call" | custom-call | tf_op jit(solution)/shard_map/soft_em/pallas_call | solution.py:306
  36.9 0.1 slice_reduce_fusion
  37.0 0.9 %multiply_convert_fusion = (bf16[128,768]{1,0:T(8,128)(2,1)}, bf16[128,768]{1,0:T(8,128)(2,1)}) fusion(f32[128,768]{1,0:T(8,128)S(1)} %get-tuple-element.9, f32[128]{0:T(128)S(1)} %slice_reduce_fusion, f32[128,768]{1,0:T(8,128)S(1)} %get-tuple-element.7), kind=kLoop, calls=%fused_computation | loop fusion | flops 393216 | bytes 1180160 | tf_op jit(solution)/shard_map/convert_element_type | solution.py:337
  37.9 0.5 %copy.8 = f32[64]{0:T(128)} copy(f32[64]{0:T(128)S(1)} %bitcast.1) | data formatting | bytes 512
